TPU v7x, 256 devices: a whole 4x4x8 slice. The times are simulated.
256 devices in a mesh: fsdp: 16 (over x, z_lo, core), replica: 16 (over y, z_hi).
Axes of the slice: x: 4, y: 4, z: 8 (z_hi: 4, z_lo: 2; z = z_hi * 2 + z_lo), core: 2. Of those that a mesh axis runs over, the one named last changes fastest.
Arguments:
- weights: float32 [256, 512, 2048], P('replica', 'fsdp'), may hold values from -0.125 to 0.125
- momentum: bfloat16 [256, 512, 2048], P('replica', 'fsdp'), may hold values from -6 to 6
- tokens: bfloat16 [229376, 2048], P(('fsdp', 'replica')), may hold values from -6 to 6
- block_expert: int32 [1792], P(('fsdp', 'replica')), may hold values from 0 to 255, as said below
- owner_expert: int32 [256], replicated, may hold values from 0 to 255, as said below
Outputs:
- fresh: bfloat16 [256, 512, 2048], P(('fsdp', 'replica'))
- rollout: bfloat16 [229376, 512], P(('fsdp', 'replica'))
Inputs may be any that keep to these rules, and one draw needn't show every extreme that they name: `owner_expert`: within each group g the entries g * N to g * N + N - 1 (N the fsdp axis size) are a permutation of the expert numbers g * N to g * N + N - 1. `block_expert`: the blocks of the device at fsdp index f and replica index r are blocks (f * R + r) * 7 to (f * R + r) * 7 + 7 - 1 (R the replica axis size). Each names an expert that owner_expert assigns to fsdp index f; the 7 blocks of one device name experts of distinct groups; in every fsdp index one group is named by every device of that index.
All inputs are finite; a program needn't handle non-finite values.
Results may differ from a plain program's by a relative error of at most 0.008.
Values may be sent and summed in bfloat16 or wider, within the bound.
A program may use at most 128 MiB of HBM per device.

v0:
```python
import math

import jax
import jax.numpy as jnp
from jax import lax
from jax.sharding import PartitionSpec as P

ROWS_E = 512
COLS = 2048
ITERS = 4


quintic_one = 3.4445
quintic_two = -4.775
quintic_three = 2.0315
learn_rate = 0.05
weight_decay = 0.1
norm_eps = 1e-07


def orthogonalize(moment):
    wide = moment.astype(jnp.float32)
    state = (wide / (jnp.sqrt(jnp.sum(wide * wide)) + norm_eps)).astype(jnp.bfloat16)
    for _ in range(ITERS):
        square = lax.dot_general(
            state, state, (((1,), (1,)), ((), ())), preferred_element_type=jnp.float32
        ).astype(jnp.bfloat16)
        twice = jnp.dot(square, square, preferred_element_type=jnp.float32)
        poly = (quintic_two * square.astype(jnp.float32) + quintic_three * twice).astype(
            jnp.bfloat16
        )
        state = (
            quintic_one * state.astype(jnp.float32)
            + jnp.dot(poly, state, preferred_element_type=jnp.float32)
        ).astype(jnp.bfloat16)
    return state


def finish(master, update):
    factor = learn_rate * 0.2 * math.sqrt(max(ROWS_E, COLS))
    return (
        master * (1.0 - learn_rate * weight_decay) - factor * update.astype(jnp.float32)
    ).astype(jnp.bfloat16)


def per_device(weights, momentum, tokens, block_expert, owner_expert):
    owners = lax.axis_size("fsdp")
    groups = lax.axis_size("replica")
    group = lax.axis_index("replica")
    table = lax.dynamic_slice_in_dim(owner_expert, group * owners, owners, 0)
    local = table - group * owners
    sent_moment = jnp.take(momentum, local, axis=0)
    sent_master = jnp.take(weights, local, axis=0)
    whole_master, whole_moment = (
        lax.all_to_all(sent_master, "fsdp", split_axis=0, concat_axis=1, tiled=True),
        lax.all_to_all(
            sent_moment.astype(jnp.float32), "fsdp", split_axis=0, concat_axis=1, tiled=True
        ),
    )
    update = orthogonalize(whole_moment[0].astype(jnp.bfloat16))
    refreshed = finish(whole_master[0], update)
    fresh = refreshed[None]
    blocks = block_expert.shape[0]
    width = tokens.shape[1]
    resident = tokens.reshape(blocks, -1, width)
    target = block_expert // owners
    selector = (target[:, None] == jnp.arange(groups, dtype=jnp.int32)[None, :]).astype(
        jnp.bfloat16
    )
    outgoing = jnp.einsum(
        "bg,brd->grd", selector, resident, preferred_element_type=jnp.float32
    ).astype(jnp.bfloat16)
    product = jnp.einsum(
        "grd,od->gro",
        lax.all_to_all(outgoing, "replica", split_axis=0, concat_axis=0, tiled=True),
        refreshed,
        preferred_element_type=jnp.float32,
    ).astype(jnp.bfloat16)
    answers = lax.all_to_all(product, "replica", split_axis=0, concat_axis=0, tiled=True)
    picked = jnp.einsum(
        "bg,gro->bro", selector, answers, preferred_element_type=jnp.float32
    ).astype(jnp.bfloat16)
    rollout = picked.reshape(-1, answers.shape[2])
    return (fresh, rollout)


def solution(mesh):
    placed = (
        P("replica", "fsdp", None),
        P("replica", "fsdp", None),
        P(("fsdp", "replica"), None),
        P(("fsdp", "replica")),
        P(),
    )
    return jax.shard_map(
        per_device,
        mesh=mesh,
        in_specs=placed,
        out_specs=(P(("fsdp", "replica"), None, None), P(("fsdp", "replica"), None)),
        check_vma=False,
    )
```

profile of v0, /device:TPU:6, one launch (start us, length us, event | category | flops | bytes accessed | tf_op | source)
XLA Modules:
  0.0 393.0 jit_solution(13910733482584841381)
XLA Ops:
  2.2 2.0 gather_fusion.1
  4.2 3.2 select_convert_fusion
  7.4 6.1 %all-to-all-start.1 = ((bf16[16,32,2048]{2,1,0:T(8,128)(2,1)}), bf16[16,32,2048]{2,1,0:T(8,128)(2,1)S(1)}, u32[]{:S(2)}, u32[]{:S(2)}) async-start(bf16[16,32,2048]{2,1,0:T(8,128)(2,1)} %select_convert_fusion), calls=%async_computation.1 | async-start | bytes 4194304 | tf_op jit(solution)/shard_map/all_to_all | solution.py:56
  13.6 5.0 %gather_fusion = f32[16,32,2048]{2,1,0:T(8,128)} fusion(f32[16,32,2048]{2,1,0:T(8,128)} %param.5, s32[1024]{0:T(1024)S(1)} %pad_clamp_fusion), kind=kCustom, calls=%fused_computation | custom fusion | bytes 8388672 | tf_op jit(solution)/shard_map/jit(_take)/gather | solution.py:53
  18.5 4.9 %broadcast_select_fusion = f32[16,32,2048]{2,1,0:T(8,128)} fusion(f32[16,32,2048]{2,1,0:T(8,128)} %gather_fusion, pred[16]{0:T(512)(128)(4,1)S(1)} %get-tuple-element.2), kind=kLoop, calls=%fused_computation.21 | loop fusion | flops 1048576 | bytes 8388624 | tf_op jit(solution)/shard_map/jit(_take)/select_n | solution.py:53
  23.4 16.3 %all-to-all-done.1 = bf16[16,32,2048]{2,1,0:T(8,128)(2,1)S(1)} async-done(((bf16[16,32,2048]{2,1,0:T(8,128)(2,1)}), bf16[16,32,2048]{2,1,0:T(8,128)(2,1)S(1)}, u32[]{:S(2)}, u32[]{:S(2)}) %all-to-all-start.1) | async-done | bytes 2097184 | tf_op jit(solution)/shard_map/all_to_all | solution.py:56
  39.8 6.1 %all-to-all-start = ((f32[16,32,2048]{2,1,0:T(8,128)}), f32[16,32,2048]{2,1,0:T(8,128)}, u32[]{:S(2)}, u32[]{:S(2)}) async-start(f32[16,32,2048]{2,1,0:T(8,128)} %broadcast_select_fusion), calls=%async_computation | async-start | bytes 8388608 | tf_op jit(solution)/shard_map/all_to_all | solution.py:55
  45.8 8.3 %convolution_convert_fusion = bf16[16,128,2048]{2,0,1:T(8,128)(2,1)} fusion(bf16[7,128,2048]{2,1,0:T(8,128)(2,1)} %bitcast.37, s32[7]{0:T(128)S(1)} %and_select_fusion), kind=kOutput, calls=%fused_computation.4 | convolution fusion | flops 62914672 | bytes 12058652 | tf_op jit(solution)/shard_map/bg,brd->grd/dot_general | solution.py:70
  54.1 11.2 %copy.13 = bf16[16,128,2048]{2,1,0:T(8,128)(2,1)} copy(bf16[16,128,2048]{2,0,1:T(8,128)(2,1)} %convolution_convert_fusion) | data formatting | bytes 16777216 | tf_op jit(solution)/shard_map/convert_element_type | solution.py:72
  65.4 29.2 %all-to-all-done = f32[16,32,2048]{2,1,0:T(8,128)} async-done(((f32[16,32,2048]{2,1,0:T(8,128)}), f32[16,32,2048]{2,1,0:T(8,128)}, u32[]{:S(2)}, u32[]{:S(2)}) %all-to-all-start) | async-done | bytes 4194336 | tf_op jit(solution)/shard_map/all_to_all | solution.py:55
  94.6 10.4 %all-to-all-start.2 = ((bf16[16,128,2048]{2,1,0:T(8,128)(2,1)}), bf16[16,128,2048]{2,1,0:T(8,128)(2,1)}, u32[]{:S(2)}, u32[]{:S(2)}) async-start(bf16[16,128,2048]{2,1,0:T(8,128)(2,1)} %copy.13), calls=%async_computation.2 | async-start | bytes 16777216 | tf_op jit(solution)/shard_map/all_to_all | solution.py:75
  105.0 1.7 fusion.2
  107.8 1.3 copy-done.2
  110.4 3.8 add_convert_fusion.3
  114.2 1.3 convolution_convert_fusion.3
  115.5 2.9 add_convert_fusion.2
  118.3 3.5 convolution_convert_fusion.2
  121.8 3.8 add_convert_fusion.1
  125.6 1.3 convolution_convert_fusion.1
  126.9 4.9 %broadcast_multiply_fusion = f32[16,32,2048]{2,1,0:T(8,128)} fusion(f32[16,32,2048]{2,1,0:T(8,128)} %all-to-all-done), kind=kLoop, calls=%fused_computation.20 | loop fusion | flops 1048576 | bytes 8388608 | tf_op jit(solution)/shard_map/mul | solution.py:42
  131.8 4.7 %fusion.4 = bf16[512,2048]{1,0:T(8,128)(2,1)} fusion(f32[16,32,2048]{2,1,0:T(8,128)} %broadcast_multiply_fusion, bf16[512,2048]{1,0:T(8,128)(2,1)S(1)} %add_convert_fusion.1, bf16[512,512]{1,0:T(8,128)(2,1)S(1)} %convolution_convert_fusion.1), kind=kOutput, calls=%fused_computation.10 | convolution fusion | flops 1351876608 | bytes 8912896 | tf_op jit(solution)/shard_map/dot_general | solution.py:34
  136.5 191.0 %all-to-all-done.2 = bf16[16,128,2048]{2,1,0:T(8,128)(2,1)} async-done(((bf16[16,128,2048]{2,1,0:T(8,128)(2,1)}), bf16[16,128,2048]{2,1,0:T(8,128)(2,1)}, u32[]{:S(2)}, u32[]{:S(2)}) %all-to-all-start.2) | async-done | bytes 8388640 | tf_op jit(solution)/shard_map/all_to_all | solution.py:75
  327.5 10.9 %fusion.9 = bf16[16,128,512]{2,0,1:T(8,128)(2,1)S(1)} fusion(bf16[512,2048]{1,0:T(8,128)(2,1)} %fusion.4, bf16[16,128,2048]{2,1,0:T(8,128)(2,1)} %all-to-all-done.2), kind=kOutput, calls=%fused_computation.22 | convolution fusion | flops 4296015872 | bytes 12582912 | tf_op jit(solution)/shard_map/grd,od->gro/dot_general | solution.py:73
  339.6 50.9 %all_to_all.28 = bf16[16,128,512]{2,1,0:T(8,128)(2,1)S(1)} all-to-all(bf16[16,128,512]{2,1,0:T(8,128)(2,1)S(1)} %copy.15), channel_id=1, replica_groups=mesh['fsdp'=16,'replica'=16] {'replica'}, dimensions={0} | all-to-all | bytes 4194304 | tf_op jit(solution)/shard_map/all_to_all | solution.py:79
  (15 shorter events, 7.0 us)
Async XLA Ops:
  0.6 1.6 copy-start
  7.4 32.3 %all-to-all-start.1 = ((bf16[16,32,2048]{2,1,0:T(8,128)(2,1)}), bf16[16,32,2048]{2,1,0:T(8,128)(2,1)S(1)}, u32[]{:S(2)}, u32[]{:S(2)}) async-start(bf16[16,32,2048]{2,1,0:T(8,128)(2,1)} %select_convert_fusion), calls=%async_computation.1 | async-start | bytes 4194304 | tf_op jit(solution)/shard_map/all_to_all | solution.py:56
  23.4 22.4 %copy-start.3 = (s32[7]{0:T(128)S(1)}, s32[7]{0:T(128)}, u32[]{:S(2)}) copy-start(s32[7]{0:T(128)} %param.8) | copy-start | bytes 88
  39.8 54.8 %all-to-all-start = ((f32[16,32,2048]{2,1,0:T(8,128)}), f32[16,32,2048]{2,1,0:T(8,128)}, u32[]{:S(2)}, u32[]{:S(2)}) async-start(f32[16,32,2048]{2,1,0:T(8,128)} %broadcast_select_fusion), calls=%async_computation | async-start | bytes 8388608 | tf_op jit(solution)/shard_map/all_to_all | solution.py:55
  94.6 232.9 %all-to-all-start.2 = ((bf16[16,128,2048]{2,1,0:T(8,128)(2,1)}), bf16[16,128,2048]{2,1,0:T(8,128)(2,1)}, u32[]{:S(2)}, u32[]{:S(2)}) async-start(bf16[16,128,2048]{2,1,0:T(8,128)(2,1)} %copy.13), calls=%async_computation.2 | async-start | bytes 16777216 | tf_op jit(solution)/shard_map/all_to_all | solution.py:75
  107.8 1.3 copy-start.2
  339.6 53.4 %copy-start.1 = (bf16[16,32,2048]{2,1,0:T(8,128)(2,1)S(1)}, bf16[16,32,2048]{2,1,0:T(8,128)(2,1)}, u32[]{:S(2)}) copy-start(bf16[16,32,2048]{2,1,0:T(8,128)(2,1)} %param.6) | copy-start | bytes 6291460
where the time goes:
time: 394 us; the launch traced here: 393 us
  waiting for transfers between devices  237 us (60%)
  blocking collectives  50.9 us (13%)
  matrix products  42.9 us (11%)
  local copies, waits for them, and re-layouts  22.6 us (6%)
  starting transfers between devices  22.6 us (6%)
  other arithmetic  16 us (4%)
    all_to_all x1, waiting for transfers between devices, per_device(): lax.all_to_all(outgoing, 'replica', split_axis=0, concat_axis=0, tiled=True)  191 us
    all_to_all x1, blocking collectives, per_device(): lax.all_to_all(product, 'replica', split_axis=0, concat_axis=0, tiled=True)  50.9 us
    all_to_all x1, waiting for transfers between devices, per_device(): lax.all_to_all(sent_master, 'fsdp', split_axis=0, concat_axis=1, tiled=True)  29.2 us
    all_to_all x1, waiting for transfers between devices, per_device(): lax.all_to_all(sent_moment.astype(jnp.float32), 'fsdp', split_axis=0, con...  16.3 us
    dot_general x4, matrix products, orthogonalize(): jnp.dot(poly, state, preferred_element_type=jnp.float32)  15.2 us
    convert_element_type x1, local copies, waits for them, and re-layouts, per_device(): outgoing = jnp.einsum('bg,brd->grd', selector, resident, preferred_elemen...  11.2 us
    dot_general x1, matrix products, per_device(): jnp.einsum('grd,od->gro', lax.all_to_all(outgoing, 'replica', split_axis=...  10.9 us
    all_to_all x1, starting transfers between devices, per_device(): lax.all_to_all(outgoing, 'replica', split_axis=0, concat_axis=0, tiled=True)  10.4 us
  transfers between devices with their start and end apart: 3, of which 3 were waited for; matrix products, arithmetic and copies ran while one was open for 15% of the time, Pallas kernels for 0%

commit v1 on v0

v1 whole, which is shorter than its diff:
```python
import math

import jax
import jax.numpy as jnp
from jax import lax
from jax.sharding import PartitionSpec as P

ITERS = 4
Z_PARTS = 4


quintic_one = 3.4445
quintic_two = -4.775
quintic_three = 2.0315
learn_rate = 0.05
weight_decay = 0.1
norm_eps = 1e-07


def orthogonalize(moment):
    wide = moment.astype(jnp.float32)
    state = (wide / (jnp.sqrt(jnp.sum(wide * wide)) + norm_eps)).astype(jnp.bfloat16)
    for _ in range(ITERS):
        square = lax.dot_general(
            state, state, (((1,), (1,)), ((), ())), preferred_element_type=jnp.float32
        ).astype(jnp.bfloat16)
        twice = jnp.dot(square, square, preferred_element_type=jnp.float32)
        poly = (quintic_two * square.astype(jnp.float32) + quintic_three * twice).astype(
            jnp.bfloat16
        )
        state = (
            quintic_one * state.astype(jnp.float32)
            + jnp.dot(poly, state, preferred_element_type=jnp.float32)
        ).astype(jnp.bfloat16)
    return state


def finish(master, update):
    rows, cols = master.shape
    factor = learn_rate * 0.2 * math.sqrt(max(rows, cols))
    return (
        master.astype(jnp.float32) * (1.0 - learn_rate * weight_decay)
        - factor * update.astype(jnp.float32)
    ).astype(jnp.bfloat16)


def per_device(weights, momentum, tokens, block_expert, owner_expert):
    owners = lax.axis_size("fsdp")
    groups = lax.axis_size("replica")
    y_parts = groups // Z_PARTS
    z_groups = [[y * Z_PARTS + z for z in range(Z_PARTS)] for y in range(y_parts)]
    y_groups = [[y * Z_PARTS + z for y in range(y_parts)] for z in range(Z_PARTS)]
    group = lax.axis_index("replica")
    table = lax.dynamic_slice_in_dim(owner_expert, group * owners, owners, 0)
    local = table - group * owners
    sent_moment = momentum.at[local].get(mode="promise_in_bounds")
    whole_moment = lax.all_to_all(sent_moment, "fsdp", split_axis=0, concat_axis=1, tiled=True)
    sent_master = weights.astype(jnp.bfloat16).at[local].get(mode="promise_in_bounds")
    whole_master = lax.all_to_all(sent_master, "fsdp", split_axis=0, concat_axis=1, tiled=True)

    blocks = block_expert.shape[0]
    width = tokens.shape[1]
    resident = tokens.reshape(blocks, -1, width)
    height = resident.shape[1]
    target = block_expert // owners
    chosen = target[None, :] == jnp.arange(groups, dtype=jnp.int32)[:, None]
    source = jnp.sum(
        jnp.where(chosen, jnp.arange(blocks, dtype=jnp.int32)[None, :], 0), axis=1
    )
    outgoing = resident.at[source].get(mode="promise_in_bounds")
    outgoing = outgoing.reshape(y_parts, Z_PARTS, height, width)
    incoming = lax.all_to_all(
        outgoing, "replica", split_axis=0, concat_axis=0, tiled=True, axis_index_groups=y_groups
    )

    update = orthogonalize(whole_moment[0])
    refreshed = finish(whole_master[0], update)
    fresh = refreshed[None]
    near = lax.all_gather(refreshed, "replica", axis_index_groups=z_groups)
    product = jnp.einsum(
        "yzrd,zod->yzro", incoming, near, preferred_element_type=jnp.float32
    ).astype(jnp.bfloat16)
    answers = lax.all_to_all(
        product, "replica", split_axis=0, concat_axis=0, tiled=True, axis_index_groups=y_groups
    )
    answers = answers.reshape(groups, height, -1)
    rollout = answers.at[target].get(mode="promise_in_bounds").reshape(blocks * height, -1)
    return (fresh, rollout)


def solution(mesh):
    placed = (
        P("replica", "fsdp", None),
        P("replica", "fsdp", None),
        P(("fsdp", "replica"), None),
        P(("fsdp", "replica")),
        P(),
    )
    return jax.shard_map(
        per_device,
        mesh=mesh,
        in_specs=placed,
        out_specs=(P(("fsdp", "replica"), None, None), P(("fsdp", "replica"), None)),
        check_vma=False,
    )
```

time: 394 us -> 298 us (0.76)
  the two profiles are of different devices: /device:TPU:6 before, /device:TPU:1 now
where the time goes in v1:
time: 298 us; the launch traced here: 297 us
  blocking collectives  101 us (34%)
  waiting for transfers between devices  98.4 us (33%)
  matrix products  31.9 us (11%)
  local copies, waits for them, and re-layouts  23.7 us (8%)
  starting transfers between devices  16.8 us (6%)
  between operations  14.8 us (5%)
  other arithmetic  11 us (4%)
    all_to_all x1, blocking collectives, per_device(): lax.all_to_all(outgoing, 'replica', split_axis=0, concat_axis=0, tiled=Tr...  101 us
    all_gather x1, waiting for transfers between devices, per_device(): near = lax.all_gather(refreshed, 'replica', axis_index_groups=z_groups)  48 us
    all_to_all x1, waiting for transfers between devices, per_device(): lax.all_to_all(product, 'replica', split_axis=0, concat_axis=0, tiled=Tru...  25.6 us
    all_to_all x1, waiting for transfers between devices, per_device(): lax.all_to_all(sent_moment, 'fsdp', split_axis=0, concat_axis=1, tiled=True)  19.5 us
    dot_general x4, matrix products, orthogonalize(): jnp.dot(poly, state, preferred_element_type=jnp.float32)  15.1 us
    dot_general x1, matrix products, per_device(): jnp.einsum('yzrd,zod->yzro', incoming, near, preferred_element_type=jnp.f...  9.45 us
    dot_general x4, matrix products, orthogonalize(): lax.dot_general(state, state, (((1,), (1,)), ((), ())), preferred_element...  7.34 us
    all_to_all x1, starting transfers between devices, per_device(): lax.all_to_all(sent_moment, 'fsdp', split_axis=0, concat_axis=1, tiled=True)  7.16 us
  transfers between devices with their start and end apart: 4, of which 4 were waited for; matrix products, arithmetic and copies ran while one was open for 11% of the time, Pallas kernels for 0%

profile of v1, /device:TPU:1, one launch (start us, length us, event | category | flops | bytes accessed | tf_op | source)
XLA Modules:
  0.0 297.2 jit_solution(5688004643062258030)
XLA Ops:
  8.8 2.0 gather_fusion.1
  10.8 7.2 %all-to-all-start.1 = ((bf16[16,32,2048]{2,1,0:T(8,128)(2,1)}), bf16[16,32,2048]{2,1,0:T(8,128)(2,1)S(1)}, u32[]{:S(2)}, u32[]{:S(2)}) async-start(bf16[16,32,2048]{2,1,0:T(8,128)(2,1)} %gather_fusion.1), calls=%async_computation.1 | async-start | bytes 4194304 | tf_op jit(solution)/shard_map/all_to_all | solution.py:57
  17.9 3.8 %convert_element_type.96 = bf16[16,32,2048]{2,1,0:T(8,128)(2,1)} convert(f32[16,32,2048]{2,1,0:T(8,128)} %param.5) | non-fusion elementwise | flops 1048576 | bytes 6291456 | tf_op jit(solution)/shard_map/convert_element_type | solution.py:58
  21.7 3.6 %gather_fusion = bf16[16,32,2048]{2,1,0:T(8,128)(2,1)} fusion(bf16[16,32,2048]{2,1,0:T(8,128)(2,1)} %convert_element_type.96, s32[1024]{0:T(1024)S(1)} %pad_clamp_fusion.2), kind=kCustom, calls=%fused_computation | custom fusion | bytes 4194368 | tf_op jit(solution)/shard_map/gather | solution.py:58
  25.4 19.5 %all-to-all-done.1 = bf16[16,32,2048]{2,1,0:T(8,128)(2,1)S(1)} async-done(((bf16[16,32,2048]{2,1,0:T(8,128)(2,1)}), bf16[16,32,2048]{2,1,0:T(8,128)(2,1)S(1)}, u32[]{:S(2)}, u32[]{:S(2)}) %all-to-all-start.1) | async-done | bytes 2097184 | tf_op jit(solution)/shard_map/all_to_all | solution.py:57
  44.9 5.1 %all-to-all-start = ((bf16[16,32,2048]{2,1,0:T(8,128)(2,1)}), bf16[16,32,2048]{2,1,0:T(8,128)(2,1)}, u32[]{:S(2)}, u32[]{:S(2)}) async-start(bf16[16,32,2048]{2,1,0:T(8,128)(2,1)} %gather_fusion), calls=%async_computation | async-start | bytes 4194304 | tf_op jit(solution)/shard_map/all_to_all | solution.py:59
  50.0 1.7 fusion.2
  52.8 1.3 copy-done.2
  55.4 3.8 %add_convert_fusion.3 = bf16[512,2048]{1,0:T(8,128)(2,1)S(1)} fusion(bf16[512,2048]{1,0:T(8,128)(2,1)} %bitcast.47, bf16[512,512]{1,0:T(8,128)(2,1)S(1)} %convolution_convert_fusion.3), kind=kOutput, calls=%fused_computation.15 | convolution fusion | flops 1347682304 | bytes 4718592 | tf_op jit(solution)/shard_map/dot_general | solution.py:33
  60.5 2.9 add_convert_fusion.2
  63.4 3.5 %convolution_convert_fusion.1 = bf16[512,512]{1,0:T(8,128)(2,1)S(1)} fusion(bf16[512,2048]{1,0:T(8,128)(2,1)} %add_convert_fusion.2), kind=kOutput, calls=%fused_computation.31 | convolution fusion | flops 1074003968 | bytes 2621440 | tf_op jit(solution)/shard_map/dot_general | solution.py:24
  66.9 3.8 %add_convert_fusion.1 = bf16[512,2048]{1,0:T(8,128)(2,1)S(1)} fusion(bf16[512,2048]{1,0:T(8,128)(2,1)} %add_convert_fusion.2, bf16[512,512]{1,0:T(8,128)(2,1)S(1)} %convolution_convert_fusion.1), kind=kOutput, calls=%fused_computation.13 | convolution fusion | flops 1347682304 | bytes 4718592 | tf_op jit(solution)/shard_map/dot_general | solution.py:33
  71.9 5.2 %all-to-all-done = bf16[16,32,2048]{2,1,0:T(8,128)(2,1)} async-done(((bf16[16,32,2048]{2,1,0:T(8,128)(2,1)}), bf16[16,32,2048]{2,1,0:T(8,128)(2,1)}, u32[]{:S(2)}, u32[]{:S(2)}) %all-to-all-start) | async-done | bytes 2097184 | tf_op jit(solution)/shard_map/all_to_all | solution.py:59
  77.1 4.1 %convert_multiply_fusion.1 = f32[16,32,2048]{2,1,0:T(8,128)} fusion(bf16[16,32,2048]{2,1,0:T(8,128)(2,1)} %all-to-all-done), kind=kLoop, calls=%fused_computation.16 | loop fusion | flops 2097152 | bytes 6291456 | tf_op jit(solution)/shard_map/mul | solution.py:42
  81.2 4.7 %fusion.4 = bf16[512,2048]{1,0:T(8,128)(2,1)} fusion(f32[16,32,2048]{2,1,0:T(8,128)} %convert_multiply_fusion.1, bf16[512,2048]{1,0:T(8,128)(2,1)S(1)} %add_convert_fusion.1, bf16[512,512]{1,0:T(8,128)(2,1)S(1)} %convolution_convert_fusion), kind=kOutput, calls=%fused_computation.11 | convolution fusion | flops 1351876608 | bytes 8912896 | tf_op jit(solution)/shard_map/dot_general | solution.py:33
  86.7 6.7 %gather_fusion.2 = bf16[16,128,2048]{2,1,0:T(8,128)(2,1)} fusion(bf16[7,128,2048]{2,1,0:T(8,128)(2,1)} %bitcast.43, s32[1024]{0:T(1024)S(1)} %pad_clamp_fusion.1), kind=kCustom, calls=%fused_computation.2 | custom fusion | bytes 16777280 | tf_op jit(solution)/shard_map/gather | solution.py:70
  93.4 100.6 %all_to_all.28 = bf16[4,4,128,2048]{3,2,1,0:T(8,128)(2,1)} all-to-all(bf16[4,4,128,2048]{3,2,1,0:T(8,128)(2,1)} %bitcast.42), channel_id=1, replica_groups={{0,4,8,12},{1,5,9,13},{2,6,10,14},{3,7,11,15},{16,20,24,28},{17,21,25,2..., dimensions={0} | all-to-all | bytes 16777216 | tf_op jit(solution)/shard_map/all_to_all | solution.py:72
  194.0 48.0 %all-gather.3.cloned.1.call-done = bf16[2048,2048]{1,0:T(8,128)(2,1)} async-done(((bf16[512,2048]{1,0:T(8,128)(2,1)}), bf16[2048,2048]{1,0:T(8,128)(2,1)}) %all-gather.3.cloned.1.call-update) | async-done | bytes 8388624 | tf_op jit(solution)/shard_map/all_gather | solution.py:79
  242.0 9.5 %convert_bitcast_fusion = bf16[4,4,128,512]{2,3,0,1:T(8,128)(2,1)S(1)} fusion(bf16[4,512,2048,1]{2,1,3,0:T(8,128)(2,1)} %bitcast.49, bf16[4,4,128,2048]{3,2,1,0:T(8,128)(2,1)} %all_to_all.28), kind=kOutput, calls=%fused_computation.17 | convolution fusion | flops 4296015872 | bytes 18874368 | tf_op jit(solution)/shard_map/yzrd,zod->yzro/dot_general | solution.py:80
  251.5 1.5 copy.13
  253.0 4.5 %all-to-all-start.3 = ((bf16[4,4,128,512]{2,3,1,0:T(8,128)(2,1)}), bf16[4,4,128,512]{2,3,1,0:T(8,128)(2,1)}, u32[]{:S(2)}, u32[]{:S(2)}) async-start(bf16[4,4,128,512]{2,3,1,0:T(8,128)(2,1)} %copy.13), calls=%async_computation.3 | async-start | bytes 4194304 | tf_op jit(solution)/shard_map/all_to_all | solution.py:83
  257.5 25.6 %all-to-all-done.3 = bf16[4,4,128,512]{2,3,1,0:T(8,128)(2,1)} async-done(((bf16[4,4,128,512]{2,3,1,0:T(8,128)(2,1)}), bf16[4,4,128,512]{2,3,1,0:T(8,128)(2,1)}, u32[]{:S(2)}, u32[]{:S(2)}) %all-to-all-start.3) | async-done | bytes 2097184 | tf_op jit(solution)/shard_map/all_to_all | solution.py:83
  283.1 4.1 %copy.14 = bf16[4,4,128,512]{3,2,1,0:T(8,128)(2,1)} copy(bf16[4,4,128,512]{2,3,1,0:T(8,128)(2,1)} %all-to-all-done.3) | data formatting | bytes 4194304 | tf_op jit(solution)/shard_map/all_to_all | solution.py:83
  287.3 3.1 %gather_fusion.3 = bf16[7,128,512]{2,1,0:T(8,128)(2,1)} fusion(bf16[16,128,512]{2,1,0:T(8,128)(2,1)} %bitcast.44, s32[1024]{0:T(1024)S(1)} %pad_clamp_fusion), kind=kCustom, calls=%fused_computation.3 | custom fusion | bytes 1835036 | tf_op jit(solution)/shard_map/gather | solution.py:87
  (20 shorter events, 6.7 us)
Async XLA Ops:
  7.2 1.6 copy-start
  10.8 34.1 %all-to-all-start.1 = ((bf16[16,32,2048]{2,1,0:T(8,128)(2,1)}), bf16[16,32,2048]{2,1,0:T(8,128)(2,1)S(1)}, u32[]{:S(2)}, u32[]{:S(2)}) async-start(bf16[16,32,2048]{2,1,0:T(8,128)(2,1)} %gather_fusion.1), calls=%async_computation.1 | async-start | bytes 4194304 | tf_op jit(solution)/shard_map/all_to_all | solution.py:57
  44.9 32.3 %all-to-all-start = ((bf16[16,32,2048]{2,1,0:T(8,128)(2,1)}), bf16[16,32,2048]{2,1,0:T(8,128)(2,1)}, u32[]{:S(2)}, u32[]{:S(2)}) async-start(bf16[16,32,2048]{2,1,0:T(8,128)(2,1)} %gather_fusion), calls=%async_computation | async-start | bytes 4194304 | tf_op jit(solution)/shard_map/all_to_all | solution.py:59
  50.0 192.0 %all-gather.3.cloned.1.call-start = ((), (), s32[]{:S(2)}) async-start(), calls=%async_computation.4 | async-start | bytes 10485760 | tf_op jit(solution)/shard_map/all_gather | solution.py:79
  52.8 1.3 copy-start.2
  85.9 0.7 copy-start.3
  253.0 30.1 %all-to-all-start.3 = ((bf16[4,4,128,512]{2,3,1,0:T(8,128)(2,1)}), bf16[4,4,128,512]{2,3,1,0:T(8,128)(2,1)}, u32[]{:S(2)}, u32[]{:S(2)}) async-start(bf16[4,4,128,512]{2,3,1,0:T(8,128)(2,1)} %copy.13), calls=%async_computation.3 | async-start | bytes 4194304 | tf_op jit(solution)/shard_map/all_to_all | solution.py:83
  257.5 32.9 %copy-start.1 = (bf16[16,32,2048]{2,1,0:T(8,128)(2,1)S(1)}, bf16[16,32,2048]{2,1,0:T(8,128)(2,1)}, u32[]{:S(2)}) copy-start(bf16[16,32,2048]{2,1,0:T(8,128)(2,1)} %param.6) | copy-start | bytes 6291460
Sparse Core Ops, SparseCore 0:
  86.1 155.9 all-gather.2

commit v2 on v1

v2 whole, which is shorter than its diff:
```python
import math

import jax
import jax.numpy as jnp
from jax import lax
from jax.experimental import pallas as pl
from jax.experimental.pallas import tpu as pltpu
from jax.sharding import PartitionSpec as P

ITERS = 4
Z_PARTS = 4
PIECES = 8
TILE = 256
MESH = pl.DeviceIdType.MESH

quintic_one = 3.4445
quintic_two = -4.775
quintic_three = 2.0315
learn_rate = 0.05
weight_decay = 0.1
norm_eps = 1e-07


def dot(left, right, transposed=False):
    dims = (((1,), (1 if transposed else 0,)), ((), ()))
    return lax.dot_general(left, right, dims, preferred_element_type=jnp.float32)


def kernel(
    block_ref,
    owner_ref,
    weights,
    momentum,
    tokens,
    fresh,
    rollout,
    mom_in,
    mas_in,
    tok_in,
    mom_out,
    mas_out,
    state,
    master,
    tok_out,
    tok_all,
    mats,
    square,
    poly,
    ans_out,
    answers,
    result,
    load_sem,
    mom_send,
    mom_recv,
    mas_send,
    mas_recv,
    tok_send,
    tok_recv,
    own_send,
    own_recv,
    fwd_send,
    fwd_recv,
    ans_send,
    ans_recv,
    store_sem,
):
    owners = lax.axis_size("fsdp")
    groups = lax.axis_size("replica")
    y_parts = groups // Z_PARTS
    rows, cols = state.shape
    shard = rows // owners
    blocks, height, _ = tok_in.shape
    f = lax.axis_index("fsdp")
    r = lax.axis_index("replica")
    y = r // Z_PARTS
    q = r - y * Z_PARTS
    left = lax.rem(q + Z_PARTS - 1, Z_PARTS)
    right = lax.rem(q + 1, Z_PARTS)
    far = lax.rem(q + 2, Z_PARTS)
    factor = learn_rate * 0.2 * math.sqrt(max(rows, cols))
    piece = rows // PIECES

    def owner_at(i):
        return lax.rem(f + i, owners)

    def y_at(i):
        return lax.rem(y + i, y_parts)

    def span(start, size):
        return pl.ds(pl.multiple_of(start * size, size), size)

    loads = [
        pltpu.make_async_copy(momentum, mom_in, load_sem.at[0]),
        pltpu.make_async_copy(weights, mas_in, load_sem.at[1]),
        pltpu.make_async_copy(tokens, tok_in, load_sem.at[2]),
    ]
    for load in loads:
        load.start()

    barrier = pltpu.get_barrier_semaphore()

    @pl.loop(1, owners)
    def _(i):
        pl.semaphore_signal(barrier, inc=1, device_id=(owner_at(i), r), device_id_type=MESH)

    for i in range(1, y_parts):
        pl.semaphore_signal(
            barrier, inc=1, device_id=(f, y_at(i) * Z_PARTS + q), device_id_type=MESH
        )
    for side in (left, right):
        pl.semaphore_signal(
            barrier, inc=1, device_id=(f, y * Z_PARTS + side), device_id_type=MESH
        )

    def local(i):
        return lax.rem(owner_ref[r * owners + i], owners)

    def mom_copy(i):
        return pltpu.make_async_remote_copy(
            src_ref=mom_out.at[i],
            dst_ref=state.at[span(f, shard)],
            send_sem=mom_send.at[i],
            recv_sem=mom_recv.at[i],
            device_id=(owner_at(i), r),
            device_id_type=MESH,
        )

    def mas_copy(i):
        return pltpu.make_async_remote_copy(
            src_ref=mas_out.at[i],
            dst_ref=master.at[span(f, shard)],
            send_sem=mas_send.at[i],
            recv_sem=mas_recv.at[i],
            device_id=(owner_at(i), r),
            device_id_type=MESH,
        )

    def tok_copy(i, k):
        return pltpu.make_async_remote_copy(
            src_ref=tok_out.at[i - 1, k],
            dst_ref=tok_all.at[k, y],
            send_sem=tok_send.at[i - 1, k],
            recv_sem=tok_recv.at[i - 1, k],
            device_id=(f, y_at(i) * Z_PARTS + q),
            device_id_type=MESH,
        )

    def own_copy(c, way):
        return pltpu.make_async_remote_copy(
            src_ref=mats.at[q, span(c, piece)],
            dst_ref=mats.at[q, span(c, piece)],
            send_sem=own_send.at[way, c],
            recv_sem=own_recv.at[way, c],
            device_id=(f, y * Z_PARTS + (right, left)[way]),
            device_id_type=MESH,
        )

    def fwd_copy(j, way):
        held = (left, right)[way]
        c = 2 * j + way
        return pltpu.make_async_remote_copy(
            src_ref=mats.at[held, span(c, piece)],
            dst_ref=mats.at[held, span(c, piece)],
            send_sem=fwd_send.at[way, j],
            recv_sem=fwd_recv.at[way, j],
            device_id=(f, y * Z_PARTS + (right, left)[way]),
            device_id_type=MESH,
        )

    def ans_copy(k, d, j, width, i):
        return pltpu.make_async_remote_copy(
            src_ref=ans_out.at[k, y_at(i), :, span(j, width)],
            dst_ref=answers.at[y * Z_PARTS + k, :, span(j, width)],
            send_sem=ans_send.at[d, j, i - 1],
            recv_sem=ans_recv.at[d, j, i - 1],
            device_id=(f, y_at(i) * Z_PARTS + q),
            device_id_type=MESH,
        )

    loads[0].wait()

    @pl.loop(1, owners)
    def _(i):
        mom_out[i] = mom_in[local(owner_at(i))]

    state[span(f, shard), :] = mom_in[local(f)]
    pl.semaphore_wait(barrier, owners - 1 + y_parts - 1 + 2)

    @pl.loop(1, owners)
    def _(i):
        mom_copy(i).start()

    loads[1].wait()

    @pl.loop(1, owners)
    def _(i):
        mas_out[i] = mas_in[local(owner_at(i))].astype(jnp.bfloat16)
        mas_copy(i).start()

    master[span(f, shard), :] = mas_in[local(f)].astype(jnp.bfloat16)

    loads[2].wait()

    def source(slot):
        found = jnp.int32(0)
        for b in range(blocks):
            found = jnp.where(lax.div(block_ref[b], owners) == slot, b, found)
        return found

    @pl.loop(0, Z_PARTS)
    def _(k):
        for i in range(1, y_parts):
            tok_out[i - 1, k] = tok_in[source(y_at(i) * Z_PARTS + k)]
            tok_copy(i, k).start()
        tok_all[k, y] = tok_in[source(y * Z_PARTS + k)]

    @pl.loop(1, owners)
    def _(i):
        mom_copy(i).wait_recv()

    def squares(i, total):
        wide = state[span(i, shard), :].astype(jnp.float32)
        return total + jnp.sum((wide * wide).reshape(shard // 8, 8, cols), axis=0)

    total = lax.fori_loop(0, owners, squares, jnp.zeros((8, cols), jnp.float32))
    inverse = 1.0 / (jnp.sqrt(jnp.sum(total, keepdims=True)) + norm_eps)

    @pl.loop(0, owners)
    def _(i):
        at = span(i, shard)
        state[at, :] = (state[at, :].astype(jnp.float32) * inverse).astype(jnp.bfloat16)

    def polynomial():
        @pl.loop(0, rows // TILE)
        def _(n):
            square[:, span(n, TILE)] = dot(state[...], state[span(n, TILE), :], True).astype(
                jnp.bfloat16
            )

        @pl.loop(0, rows // TILE)
        def _(n):
            part = square[:, span(n, TILE)]
            poly[:, span(n, TILE)] = (
                quintic_two * part.astype(jnp.float32) + quintic_three * dot(square[...], part)
            ).astype(jnp.bfloat16)

    @pl.loop(0, ITERS - 1)
    def _(step):
        polynomial()

        @pl.loop(0, cols // TILE)
        def _(n):
            part = state[:, span(n, TILE)]
            state[:, span(n, TILE)] = (
                quintic_one * part.astype(jnp.float32) + dot(poly[...], part)
            ).astype(jnp.bfloat16)

    polynomial()

    @pl.loop(1, owners)
    def _(i):
        mas_copy(i).wait_recv()

    @pl.loop(0, rows // TILE)
    def _(m):
        at = span(m, TILE)

        @pl.loop(0, cols // TILE)
        def _(n):
            cut = span(n, TILE)
            update = (
                quintic_one * state[at, cut].astype(jnp.float32)
                + dot(poly[at, :], state[:, cut])
            ).astype(jnp.bfloat16)
            mats[q, at, cut] = (
                master[at, cut].astype(jnp.float32) * (1.0 - learn_rate * weight_decay)
                - factor * update.astype(jnp.float32)
            ).astype(jnp.bfloat16)

        @pl.loop(0, PIECES * TILE // rows)
        def _(c):
            for way in (0, 1):
                own_copy(m * (PIECES * TILE // rows) + c, way).start()

    keep = pltpu.make_async_copy(mats.at[q], fresh.at[0], store_sem.at[0])
    keep.start()

    def relay(first, last):
        @pl.loop(first, last)
        def _(j):
            own_copy(2 * j, 0).wait_recv()
            fwd_copy(j, 0).start()
            own_copy(2 * j, 1).wait_recv()
            own_copy(2 * j + 1, 0).wait_recv()
            own_copy(2 * j + 1, 1).wait_recv()
            fwd_copy(j, 1).start()

    def product(k, d, j, width):
        served = dot(
            tok_all[k].reshape(y_parts * height, cols), mats[k, span(j, width), :], True
        ).astype(jnp.bfloat16)
        ans_out[k, :, :, span(j, width)] = served.reshape(y_parts, height, width)
        answers[y * Z_PARTS + k, :, span(j, width)] = ans_out[k, y, :, span(j, width)]
        for i in range(1, y_parts):
            ans_copy(k, d, j, width, i).start()

    near = rows // TILE
    thin = 2 * piece
    relay(0, PIECES // 4)

    @pl.loop(0, Z_PARTS)
    def _(k):
        for i in range(1, y_parts):
            tok_copy(i, k).wait_recv()

    @pl.loop(0, near)
    def _(j):
        product(q, 0, j, TILE)

    relay(PIECES // 4, PIECES // 2)

    @pl.loop(0, near)
    def _(j):
        product(left, 1, j, TILE)
        product(right, 2, j, TILE)

    @pl.loop(0, PIECES // 2)
    def _(j):
        fwd_copy(j, 0).wait_recv()
        fwd_copy(j, 1).wait_recv()
        product(far, 3, j, thin)

    for i in range(1, y_parts):

        @pl.loop(0, near)
        def _(j):
            for d, k in enumerate((q, left, right)):
                ans_copy(k, d, j, TILE, i).wait_recv()

        @pl.loop(0, PIECES // 2)
        def _(j):
            ans_copy(far, 3, j, thin, i).wait_recv()

    for b in range(blocks):
        result[b * height : (b + 1) * height, :] = answers[lax.div(block_ref[b], owners)]
    leave = pltpu.make_async_copy(result, rollout, store_sem.at[1])
    leave.start()

    @pl.loop(1, owners)
    def _(i):
        mom_copy(i).wait_send()
        mas_copy(i).wait_send()

    for i in range(1, y_parts):

        @pl.loop(0, Z_PARTS)
        def _(k):
            tok_copy(i, k).wait_send()

        @pl.loop(0, near)
        def _(j):
            for d, k in enumerate((q, left, right)):
                ans_copy(k, d, j, TILE, i).wait_send()

        @pl.loop(0, PIECES // 2)
        def _(j):
            ans_copy(far, 3, j, thin, i).wait_send()

    for way in (0, 1):

        @pl.loop(0, PIECES)
        def _(c):
            own_copy(c, way).wait_send()

        @pl.loop(0, PIECES // 2)
        def _(j):
            fwd_copy(j, way).wait_send()

    keep.wait()
    leave.wait()


def per_device(weights, momentum, tokens, block_expert, owner_expert):
    owners = lax.axis_size("fsdp")
    groups = lax.axis_size("replica")
    y_parts = groups // Z_PARTS
    count, shard, cols = momentum.shape
    rows = shard * owners
    blocks = block_expert.shape[0]
    height = tokens.shape[0] // blocks
    half = jnp.bfloat16
    hbm = pl.BlockSpec(memory_space=pl.ANY)
    smem = pl.BlockSpec(memory_space=pltpu.SMEM)
    dma = pltpu.SemaphoreType.DMA
    fresh, rollout = pl.pallas_call(
        kernel,
        name="muon_step",
        out_shape=(
            jax.ShapeDtypeStruct((1, rows, cols), half),
            jax.ShapeDtypeStruct((blocks * height, rows), half),
        ),
        in_specs=[smem, smem, hbm, hbm, hbm],
        out_specs=(hbm, hbm),
        scratch_shapes=[
            pltpu.VMEM((count, shard, cols), half),
            pltpu.VMEM((count, shard, cols), jnp.float32),
            pltpu.VMEM((blocks, height, cols), half),
            pltpu.VMEM((owners, shard, cols), half),
            pltpu.VMEM((owners, shard, cols), half),
            pltpu.VMEM((rows, cols), half),
            pltpu.VMEM((rows, cols), half),
            pltpu.VMEM((y_parts - 1, Z_PARTS, height, cols), half),
            pltpu.VMEM((Z_PARTS, y_parts, height, cols), half),
            pltpu.VMEM((Z_PARTS, rows, cols), half),
            pltpu.VMEM((rows, rows), half),
            pltpu.VMEM((rows, rows), half),
            pltpu.VMEM((Z_PARTS, y_parts, height, rows), half),
            pltpu.VMEM((groups, height, rows), half),
            pltpu.VMEM((blocks * height, rows), half),
            dma((3,)),
            dma((owners,)),
            dma((owners,)),
            dma((owners,)),
            dma((owners,)),
            dma((y_parts - 1, Z_PARTS)),
            dma((y_parts - 1, Z_PARTS)),
            dma((2, PIECES)),
            dma((2, PIECES)),
            dma((2, PIECES // 2)),
            dma((2, PIECES // 2)),
            dma((4, PIECES // 2, y_parts - 1)),
            dma((4, PIECES // 2, y_parts - 1)),
            dma((2,)),
        ],
        compiler_params=pltpu.CompilerParams(
            collective_id=0, has_side_effects=True, vmem_limit_bytes=60 * 2**20
        ),
    )(
        block_expert,
        owner_expert,
        weights,
        momentum,
        tokens.reshape(blocks, height, cols),
    )
    return (fresh, rollout)


def solution(mesh):
    placed = (
        P("replica", "fsdp", None),
        P("replica", "fsdp", None),
        P(("fsdp", "replica"), None),
        P(("fsdp", "replica")),
        P(),
    )
    return jax.shard_map(
        per_device,
        mesh=mesh,
        in_specs=placed,
        out_specs=(P(("fsdp", "replica"), None, None), P(("fsdp", "replica"), None)),
        check_vma=False,
    )
```

time: 298 us -> 209 us (0.70)
  Pallas kernels: 0 us -> 204 us
  blocking collectives: 101 us -> 0 us
  waiting for transfers between devices: 98.4 us -> 0 us
  matrix products: 31.9 us -> 0 us
  local copies, waits for them, and re-layouts: 23.7 us -> 4.17 us
  starting transfers between devices: 16.8 us -> 0 us
  between operations: 14.8 us -> 0.65 us
  other arithmetic: 11 us -> 0 us
    pallas_call x0 -> x1, Pallas kernels: none -> 204 us  [per_device(): pl.pallas_call(kernel, name='muon_step', out_shape=(jax.ShapeDtypeStruct(...]
    all_to_all x1 -> x0, blocking collectives: 101 us -> none  [per_device(): lax.all_to_all(outgoing, 'replica', split_axis=0, concat_axis=0, tiled=Tr...]
    all_to_all x3 -> x0, waiting for transfers between devices: 50.3 us -> none  [the longest x1 25.6 us: per_device(): lax.all_to_all(product, 'replica', split_axis=0, concat_axis=0, tiled=Tru...]
    all_gather x1 -> x0, waiting for transfers between devices: 48 us -> none  [per_device(): near = lax.all_gather(refreshed, 'replica', axis_index_groups=z_groups)]
    dot_general x9 -> x0, matrix products: 31.9 us -> none  [the longest x4 15.1 us: orthogonalize(): jnp.dot(poly, state, preferred_element_type=jnp.float32)]
    all_to_all x3 -> x0, starting transfers between devices: 16.7 us -> none  [the longest x1 7.16 us: per_device(): lax.all_to_all(sent_moment, 'fsdp', split_axis=0, concat_axis=1, tiled=True)]
    gather x4 -> x0, local copies, waits for them, and re-layouts: 15.5 us -> none  [the longest x1 6.74 us: per_device(): outgoing = resident.at[source].get(mode='promise_in_bounds')]
    convert_element_type x2 -> x0, other arithmetic: 4.23 us -> none  [the longest x1 3.83 us: per_device(): weights.astype(jnp.bfloat16).at[local].get(mode='promise_in_bounds')]
  transfers between devices with their start and end apart: 4 -> 0, of which waited for: 4 -> 0; matrix products, arithmetic and copies ran while one was open for 11% -> 0% of each run, Pallas kernels for 0% -> 0%
where the time goes in v2:
time: 209 us
  Pallas kernels  204 us (98%)
  local copies, waits for them, and re-layouts  4.17 us (2%)
    pallas_call x1, Pallas kernels, per_device(): pl.pallas_call(kernel, name='muon_step', out_shape=(jax.ShapeDtypeStruct(...  204 us

profile of v2, /device:TPU:1, one launch (start us, length us, event | category | flops | bytes accessed | tf_op | source)
XLA Modules:
  0.0 208.6 jit_solution(675513663857392860)
XLA Ops:
  0.6 203.8 %muon_step.1 = (bf16[1,512,2048]{2,1,0:T(8,128)(2,1)}, bf16[896,512]{1,0:T(8,128)(2,1)}) custom-call(s32[7]{0:T(128)} %block_ref.1, s32[256]{0:T(256)} %owner_ref.1, f32[16,32,2048]{2,1,0:T(8,128)} %weights.1, bf16[16,32,2048]{2,1,0:T(8,128)(2,1)} %momentum.1, bf16[7,128,2048]{2,1,0:T(8,128)(2,1)} %bitcast.1), custom_call_target="tpu_custom_call" | custom-call | tf_op jit(solution)/shard_map/muon_step/pallas_call | solution.py:395
  204.4 0.0 copy-start
  204.4 3.2 %copy.9 = bf16[1,512,2048]{2,1,0:T(8,128)(2,1)} copy(bf16[1,512,2048]{2,1,0:T(8,128)(2,1)} %get-tuple-element.4) | data formatting | bytes 4194304
  207.7 0.0 copy-done
  207.7 0.9 copy.10
Async XLA Ops:
  204.4 3.3 %copy-start = (bf16[896,512]{1,0:T(8,128)(2,1)S(1)}, bf16[896,512]{1,0:T(8,128)(2,1)}, u32[]{:S(2)}) copy-start(bf16[896,512]{1,0:T(8,128)(2,1)} %get-tuple-element.5) | copy-start | bytes 2752516

commit v3 on v2

--- a/solution.py
+++ b/solution.py
@@ -10,7 +10,10 @@
 ITERS = 4
 Z_PARTS = 4
 PIECES = 8
+CORES = 2
+PAIR = 2
 TILE = 256
+WIDE = 512
 MESH = pl.DeviceIdType.MESH
 
 quintic_one = 3.4445
@@ -48,7 +51,6 @@
     poly,
     ans_out,
     answers,
-    result,
     load_sem,
     mom_send,
     mom_recv,
@@ -62,7 +64,6 @@
     fwd_recv,
     ans_send,
     ans_recv,
-    store_sem,
 ):
     owners = lax.axis_size("fsdp")
     groups = lax.axis_size("replica")
@@ -80,8 +81,26 @@
     factor = learn_rate * 0.2 * math.sqrt(max(rows, cols))
     piece = rows // PIECES
 
+    inner = PAIR * CORES
+    x_parts = owners // inner
+    x = f // inner
+    z = lax.rem(f // CORES, PAIR)
+    core = lax.rem(f, CORES)
+
+    def shift(h):
+        return h + h // 2 - 2 * (h // 3)
+
+    def x_from(h):
+        return lax.rem(x + x_parts - shift(h), x_parts)
+
+    def chip_from(c):
+        return x_from(c // PAIR) * PAIR + lax.rem(z + lax.rem(c, PAIR), PAIR)
+
     def owner_at(i):
-        return lax.rem(f + i, owners)
+        c = i // CORES
+        x_to = lax.rem(x + shift(c // PAIR), x_parts)
+        z_to = lax.rem(z + lax.rem(c, PAIR), PAIR)
+        return x_to * inner + z_to * CORES + lax.rem(core + lax.rem(i, CORES), CORES)
 
     def y_at(i):
         return lax.rem(y + i, y_parts)
@@ -147,8 +166,8 @@
 
     def own_copy(c, way):
         return pltpu.make_async_remote_copy(
-            src_ref=mats.at[q, span(c, piece)],
-            dst_ref=mats.at[q, span(c, piece)],
+            src_ref=mats.at[q, span(chip_from(c), piece)],
+            dst_ref=mats.at[q, span(chip_from(c), piece)],
             send_sem=own_send.at[way, c],
             recv_sem=own_recv.at[way, c],
             device_id=(f, y * Z_PARTS + (right, left)[way]),
@@ -159,18 +178,18 @@
         held = (left, right)[way]
         c = 2 * j + way
         return pltpu.make_async_remote_copy(
-            src_ref=mats.at[held, span(c, piece)],
-            dst_ref=mats.at[held, span(c, piece)],
+            src_ref=mats.at[held, span(chip_from(c), piece)],
+            dst_ref=mats.at[held, span(chip_from(c), piece)],
             send_sem=fwd_send.at[way, j],
             recv_sem=fwd_recv.at[way, j],
             device_id=(f, y * Z_PARTS + (right, left)[way]),
             device_id_type=MESH,
         )
 
-    def ans_copy(k, d, j, width, i):
-        return pltpu.make_async_remote_copy(
-            src_ref=ans_out.at[k, y_at(i), :, span(j, width)],
-            dst_ref=answers.at[y * Z_PARTS + k, :, span(j, width)],
+    def ans_copy(k, d, j, width, i, block):
+        return pltpu.make_async_remote_copy(
+            src_ref=ans_out.at[k, y_at(i), :, span(block, width)],
+            dst_ref=answers.at[y * Z_PARTS + k, :, span(block, width)],
             send_sem=ans_send.at[d, j, i - 1],
             recv_sem=ans_recv.at[d, j, i - 1],
             device_id=(f, y_at(i) * Z_PARTS + q),
@@ -230,60 +249,45 @@
         at = span(i, shard)
         state[at, :] = (state[at, :].astype(jnp.float32) * inverse).astype(jnp.bfloat16)
 
-    def polynomial():
-        @pl.loop(0, rows // TILE)
-        def _(n):
-            square[:, span(n, TILE)] = dot(state[...], state[span(n, TILE), :], True).astype(
-                jnp.bfloat16
-            )
-
-        @pl.loop(0, rows // TILE)
-        def _(n):
-            part = square[:, span(n, TILE)]
-            poly[:, span(n, TILE)] = (
+    tiles = rows // TILE
+
+    @pl.loop(0, ITERS)
+    def _(step):
+        for n in range(tiles):
+            at = slice(n * TILE, (n + 1) * TILE)
+            square[:, at] = dot(state[...], state[at, :], True).astype(jnp.bfloat16)
+        for n in range(tiles):
+            at = slice(n * TILE, (n + 1) * TILE)
+            part = square[:, at]
+            poly[:, at] = (
                 quintic_two * part.astype(jnp.float32) + quintic_three * dot(square[...], part)
             ).astype(jnp.bfloat16)
 
-    @pl.loop(0, ITERS - 1)
-    def _(step):
-        polynomial()
-
-        @pl.loop(0, cols // TILE)
+        @pl.loop(0, cols // WIDE)
         def _(n):
-            part = state[:, span(n, TILE)]
-            state[:, span(n, TILE)] = (
+            part = state[:, span(n, WIDE)]
+            state[:, span(n, WIDE)] = (
                 quintic_one * part.astype(jnp.float32) + dot(poly[...], part)
             ).astype(jnp.bfloat16)
 
-    polynomial()
-
-    @pl.loop(1, owners)
-    def _(i):
-        mas_copy(i).wait_recv()
-
-    @pl.loop(0, rows // TILE)
-    def _(m):
-        at = span(m, TILE)
-
-        @pl.loop(0, cols // TILE)
-        def _(n):
-            cut = span(n, TILE)
-            update = (
-                quintic_one * state[at, cut].astype(jnp.float32)
-                + dot(poly[at, :], state[:, cut])
-            ).astype(jnp.bfloat16)
-            mats[q, at, cut] = (
-                master[at, cut].astype(jnp.float32) * (1.0 - learn_rate * weight_decay)
-                - factor * update.astype(jnp.float32)
-            ).astype(jnp.bfloat16)
-
-        @pl.loop(0, PIECES * TILE // rows)
-        def _(c):
-            for way in (0, 1):
-                own_copy(m * (PIECES * TILE // rows) + c, way).start()
-
-    keep = pltpu.make_async_copy(mats.at[q], fresh.at[0], store_sem.at[0])
-    keep.start()
+    def finish(c):
+        at = span(chip_from(c), piece)
+        mats[q, at, :] = (
+            master[at, :].astype(jnp.float32) * (1.0 - learn_rate * weight_decay)
+            - factor * state[at, :].astype(jnp.float32)
+        ).astype(jnp.bfloat16)
+        fresh[0, at, :] = mats[q, at, :]
+        for way in (0, 1):
+            own_copy(c, way).start()
+
+    mas_copy(1).wait_recv()
+    finish(0)
+
+    @pl.loop(1, PIECES)
+    def _(c):
+        for i in range(CORES):
+            mas_copy(CORES * c + i).wait_recv()
+        finish(c)
 
     def relay(first, last):
         @pl.loop(first, last)
@@ -295,14 +299,14 @@
             own_copy(2 * j + 1, 1).wait_recv()
             fwd_copy(j, 1).start()
 
-    def product(k, d, j, width):
+    def product(k, d, j, width, block):
         served = dot(
-            tok_all[k].reshape(y_parts * height, cols), mats[k, span(j, width), :], True
+            tok_all[k].reshape(y_parts * height, cols), mats[k, span(block, width), :], True
         ).astype(jnp.bfloat16)
-        ans_out[k, :, :, span(j, width)] = served.reshape(y_parts, height, width)
-        answers[y * Z_PARTS + k, :, span(j, width)] = ans_out[k, y, :, span(j, width)]
+        ans_out[k, :, :, span(block, width)] = served.reshape(y_parts, height, width)
+        answers[y * Z_PARTS + k, :, span(block, width)] = ans_out[k, y, :, span(block, width)]
         for i in range(1, y_parts):
-            ans_copy(k, d, j, width, i).start()
+            ans_copy(k, d, j, width, i, block).start()
 
     near = rows // TILE
     thin = 2 * piece
@@ -315,36 +319,34 @@
 
     @pl.loop(0, near)
     def _(j):
-        product(q, 0, j, TILE)
+        product(q, 0, j, TILE, j)
 
     relay(PIECES // 4, PIECES // 2)
 
     @pl.loop(0, near)
     def _(j):
-        product(left, 1, j, TILE)
-        product(right, 2, j, TILE)
+        product(left, 1, j, TILE, j)
+        product(right, 2, j, TILE, j)
 
     @pl.loop(0, PIECES // 2)
     def _(j):
         fwd_copy(j, 0).wait_recv()
         fwd_copy(j, 1).wait_recv()
-        product(far, 3, j, thin)
+        product(far, 3, j, thin, x_from(j))
 
     for i in range(1, y_parts):
 
         @pl.loop(0, near)
         def _(j):
             for d, k in enumerate((q, left, right)):
-                ans_copy(k, d, j, TILE, i).wait_recv()
+                ans_copy(k, d, j, TILE, i, j).wait_recv()
 
         @pl.loop(0, PIECES // 2)
         def _(j):
-            ans_copy(far, 3, j, thin, i).wait_recv()
+            ans_copy(far, 3, j, thin, i, x_from(j)).wait_recv()
 
     for b in range(blocks):
-        result[b * height : (b + 1) * height, :] = answers[lax.div(block_ref[b], owners)]
-    leave = pltpu.make_async_copy(result, rollout, store_sem.at[1])
-    leave.start()
+        rollout[b * height : (b + 1) * height, :] = answers[lax.div(block_ref[b], owners)]
 
     @pl.loop(1, owners)
     def _(i):
@@ -360,11 +362,11 @@
         @pl.loop(0, near)
         def _(j):
             for d, k in enumerate((q, left, right)):
-                ans_copy(k, d, j, TILE, i).wait_send()
+                ans_copy(k, d, j, TILE, i, j).wait_send()
 
         @pl.loop(0, PIECES // 2)
         def _(j):
-            ans_copy(far, 3, j, thin, i).wait_send()
+            ans_copy(far, 3, j, thin, i, x_from(j)).wait_send()
 
     for way in (0, 1):
 
@@ -375,9 +377,6 @@
         @pl.loop(0, PIECES // 2)
         def _(j):
             fwd_copy(j, way).wait_send()
-
-    keep.wait()
-    leave.wait()
 
 
 def per_device(weights, momentum, tokens, block_expert, owner_expert):
@@ -390,17 +389,18 @@
     height = tokens.shape[0] // blocks
     half = jnp.bfloat16
     hbm = pl.BlockSpec(memory_space=pl.ANY)
+    vmem = pl.BlockSpec(memory_space=pltpu.VMEM)
     smem = pl.BlockSpec(memory_space=pltpu.SMEM)
     dma = pltpu.SemaphoreType.DMA
     fresh, rollout = pl.pallas_call(
         kernel,
         name="muon_step",
         out_shape=(
-            jax.ShapeDtypeStruct((1, rows, cols), half),
-            jax.ShapeDtypeStruct((blocks * height, rows), half),
+            pltpu.VMEM((1, rows, cols), half),
+            pltpu.VMEM((blocks * height, rows), half),
         ),
         in_specs=[smem, smem, hbm, hbm, hbm],
-        out_specs=(hbm, hbm),
+        out_specs=(vmem, vmem),
         scratch_shapes=[
             pltpu.VMEM((count, shard, cols), half),
             pltpu.VMEM((count, shard, cols), jnp.float32),
@@ -416,7 +416,6 @@
             pltpu.VMEM((rows, rows), half),
             pltpu.VMEM((Z_PARTS, y_parts, height, rows), half),
             pltpu.VMEM((groups, height, rows), half),
-            pltpu.VMEM((blocks * height, rows), half),
             dma((3,)),
             dma((owners,)),
             dma((owners,)),
@@ -430,10 +429,9 @@
             dma((2, PIECES // 2)),
             dma((4, PIECES // 2, y_parts - 1)),
             dma((4, PIECES // 2, y_parts - 1)),
-            dma((2,)),
         ],
         compiler_params=pltpu.CompilerParams(
-            collective_id=0, has_side_effects=True, vmem_limit_bytes=60 * 2**20
+            collective_id=0, has_side_effects=True, vmem_limit_bytes=61 * 2**20 - 2**16
         ),
     )(
         block_expert,

time: 209 us -> 205 us (0.981)
  Pallas kernels: 204 us -> 201 us
    pallas_call x1, Pallas kernels: 204 us -> 201 us  [per_device(): pl.pallas_call(kernel, name='muon_step', out_shape=(pltpu.VMEM((1, rows,...]
where the time goes in v3:
time: 205 us; the launch traced here: 204 us
  Pallas kernels  201 us (98%)
  local copies, waits for them, and re-layouts  2.24 us (1%)
    pallas_call x1, Pallas kernels, per_device(): pl.pallas_call(kernel, name='muon_step', out_shape=(pltpu.VMEM((1, rows,...  201 us

profile of v3, /device:TPU:1, one launch (start us, length us, event | category | flops | bytes accessed | tf_op | source)
XLA Modules:
  0.0 203.6 jit_solution(18421617055530422063)
XLA Ops:
  0.6 200.7 %muon_step.1 = (bf16[1,512,2048]{2,1,0:T(8,128)(2,1)S(1)}, bf16[896,512]{1,0:T(8,128)(2,1)S(1)}) custom-call(s32[7]{0:T(128)} %block_ref.1, s32[256]{0:T(256)} %owner_ref.1, f32[16,32,2048]{2,1,0:T(8,128)} %weights.1, bf16[16,32,2048]{2,1,0:T(8,128)(2,1)} %momentum.1, bf16[7,128,2048]{2,1,0:T(8,128)(2,1)} %bitcast.1), custom_call_target="tpu_custom_call" | custom-call | tf_op jit(solution)/shard_map/muon_step/pallas_call | solution.py:395
  201.4 1.3 copy.9
  202.7 0.9 copy.10

commit v4 on v3

--- a/solution.py
+++ b/solution.py
@@ -94,12 +94,12 @@
         return lax.rem(x + x_parts - shift(h), x_parts)
 
     def chip_from(c):
-        return x_from(c // PAIR) * PAIR + lax.rem(z + lax.rem(c, PAIR), PAIR)
+        return x_from(lax.rem(c, x_parts)) * PAIR + lax.rem(z + c // x_parts, PAIR)
 
     def owner_at(i):
         c = i // CORES
-        x_to = lax.rem(x + shift(c // PAIR), x_parts)
-        z_to = lax.rem(z + lax.rem(c, PAIR), PAIR)
+        x_to = lax.rem(x + shift(lax.rem(c, x_parts)), x_parts)
+        z_to = lax.rem(z + c // x_parts, PAIR)
         return x_to * inner + z_to * CORES + lax.rem(core + lax.rem(i, CORES), CORES)
 
     def y_at(i):
@@ -176,7 +176,7 @@
 
     def fwd_copy(j, way):
         held = (left, right)[way]
-        c = 2 * j + way
+        c = j + way * (PIECES // 2)
         return pltpu.make_async_remote_copy(
             src_ref=mats.at[held, span(chip_from(c), piece)],
             dst_ref=mats.at[held, span(chip_from(c), piece)],
@@ -289,15 +289,12 @@
             mas_copy(CORES * c + i).wait_recv()
         finish(c)
 
-    def relay(first, last):
-        @pl.loop(first, last)
+    def relay(way):
+        @pl.loop(0, PIECES // 2)
         def _(j):
-            own_copy(2 * j, 0).wait_recv()
-            fwd_copy(j, 0).start()
-            own_copy(2 * j, 1).wait_recv()
-            own_copy(2 * j + 1, 0).wait_recv()
-            own_copy(2 * j + 1, 1).wait_recv()
-            fwd_copy(j, 1).start()
+            for side in (0, 1):
+                own_copy(j + way * (PIECES // 2), side).wait_recv()
+            fwd_copy(j, way).start()
 
     def product(k, d, j, width, block):
         served = dot(
@@ -310,7 +307,7 @@
 
     near = rows // TILE
     thin = 2 * piece
-    relay(0, PIECES // 4)
+    relay(0)
 
     @pl.loop(0, Z_PARTS)
     def _(k):
@@ -321,25 +318,49 @@
     def _(j):
         product(q, 0, j, TILE, j)
 
-    relay(PIECES // 4, PIECES // 2)
+    relay(1)
 
     @pl.loop(0, near)
     def _(j):
         product(left, 1, j, TILE, j)
         product(right, 2, j, TILE, j)
 
-    @pl.loop(0, PIECES // 2)
+    def serve_far(j):
+        for way in (0, 1):
+            fwd_copy(j, way).wait_recv()
+        product(far, 3, j, thin, x_from(j))
+
+    last = PIECES // 2 - 1
+
+    @pl.loop(0, last)
     def _(j):
-        fwd_copy(j, 0).wait_recv()
-        fwd_copy(j, 1).wait_recv()
-        product(far, 3, j, thin, x_from(j))
+        serve_far(j)
+
+    @pl.loop(1, owners)
+    def _(i):
+        mom_copy(i).wait_send()
+        mas_copy(i).wait_send()
 
     for i in range(1, y_parts):
+
+        @pl.loop(0, Z_PARTS)
+        def _(k):
+            tok_copy(i, k).wait_send()
 
         @pl.loop(0, near)
         def _(j):
             for d, k in enumerate((q, left, right)):
-                ans_copy(k, d, j, TILE, i, j).wait_recv()
+                ans_copy(k, d, j, TILE, i, j).wait()
+
+    for way in (0, 1):
+
+        @pl.loop(0, PIECES)
+        def _(c):
+            own_copy(c, way).wait_send()
+
+    serve_far(last)
+
+    for i in range(1, y_parts):
 
         @pl.loop(0, PIECES // 2)
         def _(j):
@@ -348,31 +369,13 @@
     for b in range(blocks):
         rollout[b * height : (b + 1) * height, :] = answers[lax.div(block_ref[b], owners)]
 
-    @pl.loop(1, owners)
-    def _(i):
-        mom_copy(i).wait_send()
-        mas_copy(i).wait_send()
-
     for i in range(1, y_parts):
-
-        @pl.loop(0, Z_PARTS)
-        def _(k):
-            tok_copy(i, k).wait_send()
-
-        @pl.loop(0, near)
-        def _(j):
-            for d, k in enumerate((q, left, right)):
-                ans_copy(k, d, j, TILE, i, j).wait_send()
 
         @pl.loop(0, PIECES // 2)
         def _(j):
             ans_copy(far, 3, j, thin, i, x_from(j)).wait_send()
 
     for way in (0, 1):
-
-        @pl.loop(0, PIECES)
-        def _(c):
-            own_copy(c, way).wait_send()
 
         @pl.loop(0, PIECES // 2)
         def _(j):

time: 205 us -> 203 us (level)
  no operation moved by 1% of the time
where the time goes in v4:
time: 203 us
  Pallas kernels  200 us (99%)
  local copies, waits for them, and re-layouts  2.24 us (1%)
    pallas_call x1, Pallas kernels, per_device(): pl.pallas_call(kernel, name='muon_step', out_shape=(pltpu.VMEM((1, rows,...  200 us

profile of v4, /device:TPU:1, one launch (start us, length us, event | category | flops | bytes accessed | tf_op | source)
XLA Modules:
  0.0 202.7 jit_solution(13789234045870922278)
XLA Ops:
  0.6 199.9 %muon_step.1 = (bf16[1,512,2048]{2,1,0:T(8,128)(2,1)S(1)}, bf16[896,512]{1,0:T(8,128)(2,1)S(1)}) custom-call(s32[7]{0:T(128)} %block_ref.1, s32[256]{0:T(256)} %owner_ref.1, f32[16,32,2048]{2,1,0:T(8,128)} %weights.1, bf16[16,32,2048]{2,1,0:T(8,128)(2,1)} %momentum.1, bf16[7,128,2048]{2,1,0:T(8,128)(2,1)} %bitcast.1), custom_call_target="tpu_custom_call" | custom-call | tf_op jit(solution)/shard_map/muon_step/pallas_call | solution.py:398
  200.5 1.3 copy.9
  201.8 0.9 copy.10
